TPU v7x, 32 devices: a whole 2x2x4 slice. The times are simulated.
32 devices in a mesh: row: 4 (over x, core), col: 8 (over z, y).
Axes of the slice: x: 2, y: 2, z: 4, core: 2. Of those that a mesh axis runs over, the one named last changes fastest.
Arguments:
- x_vals: bfloat16 [256, 32, 4096], P(('row', 'col')), may hold values from -6 to 6
- occupancy: int32 [256, 32], P(('row', 'col')), may hold values from 0 to 1, as said below
- perm: int32 [256], replicated, may hold values from 0 to 255, as said below
Outputs:
- sign_iterate_next: bfloat16 [16384, 16384], P('row', 'col')
Inputs may be any that keep to these rules, and one draw needn't show every extreme that they name: occupancy[i, s] = 1 marks block (i, (i - 16 + s) mod 256) as present; the diagonal slot s = 16 is always 1, and some row has all 32 slots 1. perm is a permutation with perm[j] = a(j mod (8)) * 32 + b(j div (8)) for permutations a and b; so the 32 band columns of any row fall exactly 4 times into each aligned run of 32 new indices, and each aligned run of 64 initial indices has exactly 16 members in each aligned run of 64 new indices.
All inputs are finite; a program needn't handle non-finite values.
Results may differ from a plain program's by a relative error of at most 0.0017.
Values may be sent and summed in bfloat16 or wider, within the bound.
A program may use at most 128 MiB of HBM per device.

v0:
```python
import math
import jax
import jax.numpy as jnp
from jax import lax
from jax.sharding import PartitionSpec as P

BLOCK_EDGE = 64


def bucket_slots(x_vals, occupancy, perm, first_row, column_processors, tile_slots):
    local_rows, band_extent = occupancy.shape
    block_count = perm.shape[0]
    panel_cols = block_count // column_processors
    row_ids = first_row + jnp.arange(local_rows, dtype=jnp.int32)
    orig_cols = (
        row_ids[:, None] - band_extent // 2 + jnp.arange(band_extent, dtype=jnp.int32)[None, :]
    ) % block_count
    new_cols = perm[orig_cols]
    panel_of = new_cols // panel_cols
    inside = new_cols % panel_cols
    in_panel = (
        (occupancy[:, :, None] == 1)
        & (panel_of[:, :, None] == jnp.arange(column_processors)[None, None, :])
    ).astype(jnp.int32)
    before = jnp.cumsum(in_panel, axis=1) - in_panel
    slot_rank = jnp.sum(before * in_panel, axis=2)
    placed = in_panel[:, :, :, None] * (
        slot_rank[:, :, None, None] == jnp.arange(tile_slots)[None, None, None, :]
    ).astype(jnp.int32)
    values = jnp.einsum(
        "kspt,ksf->pktf", placed.astype(jnp.bfloat16), x_vals, preferred_element_type=jnp.float32
    ).astype(jnp.bfloat16)
    columns = jnp.einsum("kspt,ks->pkt", placed, inside + 1) - 1
    return (values, columns)


def filtered_product(row_vals, row_cols, far_vals, far_cols, tile_cols, panel_cols):
    panel_rows, tile_slots = tile_cols.shape
    panel_count = row_vals.shape[0]
    block_area = row_vals.shape[3]
    group = math.gcd(panel_count, max(1, 16 // (tile_slots * tile_slots)))
    wanted = tile_cols >= 0

    def one_group(running, inputs):
        panel_index, piece_vals, piece_cols = inputs
        present_mask = piece_cols >= 0
        source = jnp.where(present_mask, panel_index[:, None, None] * panel_cols + piece_cols, 0)
        found_cols = far_cols[source]
        whole_rows = far_vals[source]
        chosen = jnp.zeros((group, panel_rows, tile_slots, tile_slots, block_area), far_vals.dtype)
        for slot in range(tile_slots):
            hit = (
                (found_cols[:, :, :, slot][:, :, :, None] == tile_cols[None, :, None, :])
                & present_mask[:, :, :, None]
                & wanted[None, :, None, :]
            )
            chosen = jnp.where(
                hit[:, :, :, :, None], whole_rows[:, :, :, slot][:, :, :, None, :], chosen
            )
        left_factor_blocks = piece_vals.reshape(
            group, panel_rows, tile_slots, BLOCK_EDGE, BLOCK_EDGE
        )
        right_factor_blocks = chosen.reshape(
            group, panel_rows, tile_slots, tile_slots, BLOCK_EDGE, BLOCK_EDGE
        )
        update = jnp.einsum(
            "givab,givubc->iuac",
            left_factor_blocks,
            right_factor_blocks,
            preferred_element_type=jnp.float32,
        )
        return (running + update, None)

    start = jnp.zeros((panel_rows, tile_slots, BLOCK_EDGE, BLOCK_EDGE), jnp.float32)
    panel_ids = jnp.arange(panel_count, dtype=jnp.int32).reshape(panel_count // group, group)
    grouped_vals = row_vals.reshape(panel_count // group, group, panel_rows, tile_slots, block_area)
    grouped_cols = row_cols.reshape(panel_count // group, group, panel_rows, tile_slots)
    running, _ = lax.scan(one_group, start, (panel_ids, grouped_vals, grouped_cols))
    return running.reshape(panel_rows, tile_slots, BLOCK_EDGE * BLOCK_EDGE)


def shards(x_vals, occupancy, perm):
    row_devices = lax.axis_size("row")
    column_processors = lax.axis_size("col")
    own_row = lax.axis_index("row")
    own_col = lax.axis_index("col")
    local_rows = x_vals.shape[0]
    band_extent = x_vals.shape[1]
    block_area = x_vals.shape[2]
    block_count = perm.shape[0]
    panel_rows = block_count // row_devices
    panel_cols = block_count // column_processors
    tile_slots = band_extent // column_processors
    first_row = (own_row * column_processors + own_col) * local_rows
    values, columns = bucket_slots(
        x_vals, occupancy, perm, first_row, column_processors, tile_slots
    )
    first_vals, first_cols = (
        lax.all_to_all(values, "col", split_axis=0, concat_axis=0, tiled=True),
        lax.all_to_all(
            columns.astype(jnp.bfloat16), "col", split_axis=0, concat_axis=0, tiled=True
        ),
    )
    first_vals = first_vals.reshape(panel_rows, tile_slots, block_area)
    first_cols = first_cols.astype(jnp.int32).reshape(panel_rows, tile_slots)
    group_new = lax.dynamic_slice_in_dim(perm, own_row * panel_rows, panel_rows) // panel_rows
    per_panel = panel_rows // row_devices
    heading = (group_new[:, None] == jnp.arange(row_devices)[None, :]).astype(jnp.int32)
    ahead = jnp.cumsum(heading, axis=0) - heading
    order_in = jnp.sum(ahead * heading, axis=1)
    placed = heading[:, :, None] * (
        order_in[:, None, None] == jnp.arange(per_panel)[None, None, :]
    ).astype(jnp.int32)
    send_vals = jnp.einsum(
        "gre,gtf->retf", placed.astype(jnp.bfloat16), first_vals, preferred_element_type=jnp.float32
    ).astype(jnp.bfloat16)
    send_cols = (jnp.einsum("gre,gt->ret", placed, first_cols + 1) - 1).astype(jnp.bfloat16)
    got_vals, got_cols = (
        lax.all_to_all(send_vals, "row", split_axis=0, concat_axis=0, tiled=True),
        lax.all_to_all(send_cols, "row", split_axis=0, concat_axis=0, tiled=True),
    )
    got_vals = got_vals.reshape(panel_rows, tile_slots * block_area)
    got_cols = got_cols.astype(jnp.int32).reshape(panel_rows, tile_slots)
    every_new = perm.reshape(row_devices, panel_rows)
    landing = (every_new // panel_rows == own_row).astype(jnp.int32)
    earlier = jnp.cumsum(landing, axis=1) - landing
    arrival = landing[:, :, None] * (
        earlier[:, :, None] == jnp.arange(per_panel)[None, None, :]
    ).astype(jnp.int32)
    target_row = (
        (every_new - own_row * panel_rows)[:, :, None] == jnp.arange(panel_rows)[None, None, :]
    ).astype(jnp.int32)
    selector = jnp.einsum("sge,sgl->lse", arrival, target_row).reshape(panel_rows, panel_rows)
    tile_vals = jnp.dot(
        selector.astype(jnp.bfloat16), got_vals, preferred_element_type=jnp.float32
    ).astype(jnp.bfloat16)
    tile_vals = tile_vals.reshape(panel_rows, tile_slots, block_area)
    tile_cols = jnp.dot(selector, got_cols + 1) - 1
    cols_wire = tile_cols.astype(jnp.bfloat16)
    row_vals, row_cols = (
        lax.all_gather(tile_vals[None], "col", axis=0, tiled=True),
        lax.all_gather(cols_wire[None], "col", axis=0, tiled=True),
    )
    row_cols = row_cols.astype(jnp.int32)
    far_vals, far_cols = (
        lax.all_gather(tile_vals, "row", axis=0, tiled=True),
        lax.all_gather(cols_wire, "row", axis=0, tiled=True),
    )
    far_cols = far_cols.astype(jnp.int32)
    square = filtered_product(row_vals, row_cols, far_vals, far_cols, tile_cols, panel_cols).astype(
        jnp.bfloat16
    )
    far_square = lax.all_gather(square, "row", axis=0, tiled=True)
    cube_vals = filtered_product(row_vals, row_cols, far_square, far_cols, tile_cols, panel_cols)
    stepped_matrix = (
        1.5 * tile_vals.astype(jnp.float32) - 0.5 / (BLOCK_EDGE * band_extent) * cube_vals
    )
    spread = (tile_cols[:, :, None] == jnp.arange(panel_cols)[None, None, :]).astype(jnp.float32)
    dense_tile = jnp.einsum(
        "iuj,iuac->iajc",
        spread,
        stepped_matrix.reshape(panel_rows, tile_slots, BLOCK_EDGE, BLOCK_EDGE),
    )
    return dense_tile.reshape(panel_rows * BLOCK_EDGE, panel_cols * BLOCK_EDGE).astype(jnp.bfloat16)


def solution(mesh):
    return jax.shard_map(
        shards,
        mesh=mesh,
        in_specs=(P(("row", "col"), None, None), P(("row", "col"), None), P()),
        out_specs=P("row", "col"),
        check_vma=False,
    )
```

profile of v0, /device:TPU:0, one launch (start us, length us, event | category | flops | bytes accessed | tf_op | source)
XLA Modules:
  0.0 2926.6 jit_solution(10407044865748420455)
XLA Ops:
  21.5 47.9 %all-to-all-done = bf16[8,8,4,4096]{3,2,1,0:T(4,128)(2,1)} async-done(((bf16[8,8,4,4096]{3,2,1,0:T(4,128)(2,1)}), bf16[8,8,4,4096]{3,2,1,0:T(4,128)(2,1)}, u32[]{:S(2)}, u32[]{:S(2)}) %all-to-all-start) | async-done | bytes 2097184 | tf_op jit(solution)/shard_map/all_to_all | solution.py:99
  80.5 24.8 all-to-all-done.1
  125.3 10.7 all_to_all.20
  144.5 17.9 all-gather.1
  167.9 177.1 %all-gather.9.cloned.1.call-done = bf16[8,64,4,4096]{3,1,2,0:T(8,128)(2,1)} async-done(((bf16[1,64,4,4096]{3,1,2,0:T(8,128)(2,1)}), bf16[8,64,4,4096]{3,1,2,0:T(8,128)(2,1)}) %all-gather.9.cloned.1.call-update) | async-done | bytes 16777232 | tf_op jit(solution)/shard_map/all_gather | solution.py:141
  345.0 22.2 copy.185
  367.2 35.8 %all-gather.7.cloned.1.call-done = bf16[256,4,4096]{2,1,0:T(4,128)(2,1)} async-done(((bf16[64,4,4096]{2,1,0:T(4,128)(2,1)}), bf16[256,4,4096]{2,1,0:T(4,128)(2,1)}) %all-gather.7.cloned.1.call-update) | async-done | bytes 8388624 | tf_op jit(solution)/shard_map/all_gather | solution.py:146
  403.0 1186.4 %while.22 = (s32[]{:T(128)}, f32[64,4,64,64]{2,3,1,0:T(8,128)}, s32[8,1,64,4]{3,2,1,0:T(8,128)S(1)}, s32[8,1]{0,1:T(1,128)S(1)}, s32[256,4]{1,0:T(8,128)S(1)}, /...) while((s32[]{:T(128)}, f32[64,4,64,64]{2,3,1,0:T(8,128)}, ...), condition=%wide.region_6.7_spmd.clone, body=%wide.region_5.6_spmd.clone.sunk | while | flops 555760128 | bytes 94430096 | solution.py:78
  421.9 16.1 gather_fusion.1
  438.1 47.0 %slice_reduce_fusion.10 = (bf16[64,4,4096]{2,1,0:T(4,128)(2,1)}, bf16[64,4,4096]{2,1,0:T(4,128)(2,1)}, bf16[64,4,4096]{2,1,0:T(4,128)(2,1)}, bf16[64,4,4096]{2,1,0:T(4,128)(2,1)}) fusion(bf16[1,64,4,4,4096]{4,3,2,1,0:T(4,128)(2,1)} %bitcast.158), kind=kLoop, calls=%fused_computation.23.clone.1 | loop fusion | bytes 16777216 | tf_op jit(solution)/shard_map/while/body/eval_jaxpr/slice | solution.py:58
  549.9 13.5 bitcast_add_fusion.5
  566.9 16.1 gather_fusion.1
  583.0 47.0 %slice_reduce_fusion.10 = (bf16[64,4,4096]{2,1,0:T(4,128)(2,1)}, bf16[64,4,4096]{2,1,0:T(4,128)(2,1)}, bf16[64,4,4096]{2,1,0:T(4,128)(2,1)}, bf16[64,4,4096]{2,1,0:T(4,128)(2,1)}) fusion(bf16[1,64,4,4,4096]{4,3,2,1,0:T(4,128)(2,1)} %bitcast.158), kind=kLoop, calls=%fused_computation.23.clone.1 | loop fusion | bytes 16777216 | tf_op jit(solution)/shard_map/while/body/eval_jaxpr/slice | solution.py:58
  694.9 15.1 bitcast_add_fusion.5
  713.4 16.1 gather_fusion.1
  729.6 47.0 %slice_reduce_fusion.10 = (bf16[64,4,4096]{2,1,0:T(4,128)(2,1)}, bf16[64,4,4096]{2,1,0:T(4,128)(2,1)}, bf16[64,4,4096]{2,1,0:T(4,128)(2,1)}, bf16[64,4,4096]{2,1,0:T(4,128)(2,1)}) fusion(bf16[1,64,4,4,4096]{4,3,2,1,0:T(4,128)(2,1)} %bitcast.158), kind=kLoop, calls=%fused_computation.23.clone.1 | loop fusion | bytes 16777216 | tf_op jit(solution)/shard_map/while/body/eval_jaxpr/slice | solution.py:58
  841.4 15.1 bitcast_add_fusion.5
  860.0 16.2 gather_fusion.1
  876.1 47.0 %slice_reduce_fusion.10 = (bf16[64,4,4096]{2,1,0:T(4,128)(2,1)}, bf16[64,4,4096]{2,1,0:T(4,128)(2,1)}, bf16[64,4,4096]{2,1,0:T(4,128)(2,1)}, bf16[64,4,4096]{2,1,0:T(4,128)(2,1)}) fusion(bf16[1,64,4,4,4096]{4,3,2,1,0:T(4,128)(2,1)} %bitcast.158), kind=kLoop, calls=%fused_computation.23.clone.1 | loop fusion | bytes 16777216 | tf_op jit(solution)/shard_map/while/body/eval_jaxpr/slice | solution.py:58
  988.0 15.1 bitcast_add_fusion.5
  1006.5 16.1 gather_fusion.1
  1022.6 47.0 %slice_reduce_fusion.10 = (bf16[64,4,4096]{2,1,0:T(4,128)(2,1)}, bf16[64,4,4096]{2,1,0:T(4,128)(2,1)}, bf16[64,4,4096]{2,1,0:T(4,128)(2,1)}, bf16[64,4,4096]{2,1,0:T(4,128)(2,1)}) fusion(bf16[1,64,4,4,4096]{4,3,2,1,0:T(4,128)(2,1)} %bitcast.158), kind=kLoop, calls=%fused_computation.23.clone.1 | loop fusion | bytes 16777216 | tf_op jit(solution)/shard_map/while/body/eval_jaxpr/slice | solution.py:58
  1134.5 15.1 bitcast_add_fusion.5
  1153.0 16.1 gather_fusion.1
  1169.1 47.0 %slice_reduce_fusion.10 = (bf16[64,4,4096]{2,1,0:T(4,128)(2,1)}, bf16[64,4,4096]{2,1,0:T(4,128)(2,1)}, bf16[64,4,4096]{2,1,0:T(4,128)(2,1)}, bf16[64,4,4096]{2,1,0:T(4,128)(2,1)}) fusion(bf16[1,64,4,4,4096]{4,3,2,1,0:T(4,128)(2,1)} %bitcast.158), kind=kLoop, calls=%fused_computation.23.clone.1 | loop fusion | bytes 16777216 | tf_op jit(solution)/shard_map/while/body/eval_jaxpr/slice | solution.py:58
  1281.0 15.1 bitcast_add_fusion.5
  1299.5 16.2 gather_fusion.1
  1315.7 47.0 %slice_reduce_fusion.10 = (bf16[64,4,4096]{2,1,0:T(4,128)(2,1)}, bf16[64,4,4096]{2,1,0:T(4,128)(2,1)}, bf16[64,4,4096]{2,1,0:T(4,128)(2,1)}, bf16[64,4,4096]{2,1,0:T(4,128)(2,1)}) fusion(bf16[1,64,4,4,4096]{4,3,2,1,0:T(4,128)(2,1)} %bitcast.158), kind=kLoop, calls=%fused_computation.23.clone.1 | loop fusion | bytes 16777216 | tf_op jit(solution)/shard_map/while/body/eval_jaxpr/slice | solution.py:58
  1427.5 15.1 bitcast_add_fusion.5
  1446.1 16.1 gather_fusion.1
  1462.2 47.0 %slice_reduce_fusion.10 = (bf16[64,4,4096]{2,1,0:T(4,128)(2,1)}, bf16[64,4,4096]{2,1,0:T(4,128)(2,1)}, bf16[64,4,4096]{2,1,0:T(4,128)(2,1)}, bf16[64,4,4096]{2,1,0:T(4,128)(2,1)}) fusion(bf16[1,64,4,4,4096]{4,3,2,1,0:T(4,128)(2,1)} %bitcast.158), kind=kLoop, calls=%fused_computation.23.clone.1 | loop fusion | bytes 16777216 | tf_op jit(solution)/shard_map/while/body/eval_jaxpr/slice | solution.py:58
  1574.0 15.1 bitcast_add_fusion.5
  1609.4 7.3 mul.90
  1616.7 9.4 copy.192
  1626.1 41.7 %all-gather.11.cloned.1.call-done = bf16[256,4,4096]{2,1,0:T(4,128)(2,1)} async-done(((bf16[64,4,4096]{2,1,0:T(4,128)(2,1)}), bf16[256,4,4096]{2,1,0:T(4,128)(2,1)}) %all-gather.11.cloned.1.call-update) | async-done | bytes 8388624 | tf_op jit(solution)/shard_map/all_gather | solution.py:153
  1667.8 1172.4 %while.23 = (s32[]{:T(128)}, f32[64,4,64,64]{2,3,1,0:T(8,128)}, s32[8,1,64,4]{3,2,1,0:T(8,128)S(1)}, s32[8,1]{0,1:T(1,128)S(1)}, s32[256,4]{1,0:T(8,128)S(1)}, /...) while((s32[]{:T(128)}, f32[64,4,64,64]{2,3,1,0:T(8,128)}, ...), condition=%wide.region_8.9_spmd.clone, body=%wide.region_7.8_spmd.clone.sunk | while | flops 555760128 | bytes 94430096 | solution.py:78
  1671.5 16.1 gather_fusion.3
  1687.6 47.3 %slice_reduce_fusion.11 = (bf16[64,4,4096]{2,1,0:T(4,128)(2,1)}, bf16[64,4,4096]{2,1,0:T(4,128)(2,1)}, bf16[64,4,4096]{2,1,0:T(4,128)(2,1)}, bf16[64,4,4096]{2,1,0:T(4,128)(2,1)}) fusion(bf16[1,64,4,4,4096]{4,3,2,1,0:T(4,128)(2,1)} %bitcast.159), kind=kLoop, calls=%fused_computation.53.clone.1 | loop fusion | bytes 16777216 | tf_op jit(solution)/shard_map/while/body/eval_jaxpr/slice | solution.py:58
  1799.6 13.5 bitcast_add_fusion.6
  1816.6 16.1 gather_fusion.3
  1832.7 47.3 %slice_reduce_fusion.11 = (bf16[64,4,4096]{2,1,0:T(4,128)(2,1)}, bf16[64,4,4096]{2,1,0:T(4,128)(2,1)}, bf16[64,4,4096]{2,1,0:T(4,128)(2,1)}, bf16[64,4,4096]{2,1,0:T(4,128)(2,1)}) fusion(bf16[1,64,4,4,4096]{4,3,2,1,0:T(4,128)(2,1)} %bitcast.159), kind=kLoop, calls=%fused_computation.53.clone.1 | loop fusion | bytes 16777216 | tf_op jit(solution)/shard_map/while/body/eval_jaxpr/slice | solution.py:58
  1944.7 15.1 bitcast_add_fusion.6
  1963.3 16.1 gather_fusion.3
  1979.4 47.3 %slice_reduce_fusion.11 = (bf16[64,4,4096]{2,1,0:T(4,128)(2,1)}, bf16[64,4,4096]{2,1,0:T(4,128)(2,1)}, bf16[64,4,4096]{2,1,0:T(4,128)(2,1)}, bf16[64,4,4096]{2,1,0:T(4,128)(2,1)}) fusion(bf16[1,64,4,4,4096]{4,3,2,1,0:T(4,128)(2,1)} %bitcast.159), kind=kLoop, calls=%fused_computation.53.clone.1 | loop fusion | bytes 16777216 | tf_op jit(solution)/shard_map/while/body/eval_jaxpr/slice | solution.py:58
  2091.4 15.1 bitcast_add_fusion.6
  2110.0 16.1 gather_fusion.3
  2126.1 47.3 %slice_reduce_fusion.11 = (bf16[64,4,4096]{2,1,0:T(4,128)(2,1)}, bf16[64,4,4096]{2,1,0:T(4,128)(2,1)}, bf16[64,4,4096]{2,1,0:T(4,128)(2,1)}, bf16[64,4,4096]{2,1,0:T(4,128)(2,1)}) fusion(bf16[1,64,4,4,4096]{4,3,2,1,0:T(4,128)(2,1)} %bitcast.159), kind=kLoop, calls=%fused_computation.53.clone.1 | loop fusion | bytes 16777216 | tf_op jit(solution)/shard_map/while/body/eval_jaxpr/slice | solution.py:58
  2238.2 15.1 bitcast_add_fusion.6
  2256.7 16.1 gather_fusion.3
  2272.8 47.3 %slice_reduce_fusion.11 = (bf16[64,4,4096]{2,1,0:T(4,128)(2,1)}, bf16[64,4,4096]{2,1,0:T(4,128)(2,1)}, bf16[64,4,4096]{2,1,0:T(4,128)(2,1)}, bf16[64,4,4096]{2,1,0:T(4,128)(2,1)}) fusion(bf16[1,64,4,4,4096]{4,3,2,1,0:T(4,128)(2,1)} %bitcast.159), kind=kLoop, calls=%fused_computation.53.clone.1 | loop fusion | bytes 16777216 | tf_op jit(solution)/shard_map/while/body/eval_jaxpr/slice | solution.py:58
  2384.8 15.1 bitcast_add_fusion.6
  2403.4 16.1 gather_fusion.3
  2419.5 47.3 %slice_reduce_fusion.11 = (bf16[64,4,4096]{2,1,0:T(4,128)(2,1)}, bf16[64,4,4096]{2,1,0:T(4,128)(2,1)}, bf16[64,4,4096]{2,1,0:T(4,128)(2,1)}, bf16[64,4,4096]{2,1,0:T(4,128)(2,1)}) fusion(bf16[1,64,4,4,4096]{4,3,2,1,0:T(4,128)(2,1)} %bitcast.159), kind=kLoop, calls=%fused_computation.53.clone.1 | loop fusion | bytes 16777216 | tf_op jit(solution)/shard_map/while/body/eval_jaxpr/slice | solution.py:58
  2531.5 15.1 bitcast_add_fusion.6
  2550.1 16.1 gather_fusion.3
  2566.2 47.3 %slice_reduce_fusion.11 = (bf16[64,4,4096]{2,1,0:T(4,128)(2,1)}, bf16[64,4,4096]{2,1,0:T(4,128)(2,1)}, bf16[64,4,4096]{2,1,0:T(4,128)(2,1)}, bf16[64,4,4096]{2,1,0:T(4,128)(2,1)}) fusion(bf16[1,64,4,4,4096]{4,3,2,1,0:T(4,128)(2,1)} %bitcast.159), kind=kLoop, calls=%fused_computation.53.clone.1 | loop fusion | bytes 16777216 | tf_op jit(solution)/shard_map/while/body/eval_jaxpr/slice | solution.py:58
  2678.2 15.1 bitcast_add_fusion.6
  2696.8 16.1 gather_fusion.3
  2712.9 47.3 %slice_reduce_fusion.11 = (bf16[64,4,4096]{2,1,0:T(4,128)(2,1)}, bf16[64,4,4096]{2,1,0:T(4,128)(2,1)}, bf16[64,4,4096]{2,1,0:T(4,128)(2,1)}, bf16[64,4,4096]{2,1,0:T(4,128)(2,1)}) fusion(bf16[1,64,4,4,4096]{4,3,2,1,0:T(4,128)(2,1)} %bitcast.159), kind=kLoop, calls=%fused_computation.53.clone.1 | loop fusion | bytes 16777216 | tf_op jit(solution)/shard_map/while/body/eval_jaxpr/slice | solution.py:58
  2824.9 15.1 bitcast_add_fusion.6
  2840.2 10.0 multiply_subtract_fusion
  2850.2 7.5 copy.194
  2857.6 16.1 convert_bitcast_fusion
  2873.7 46.0 %convert_element_type.138 = bf16[4096,2048]{1,0:T(8,128)(2,1)} reshape(bf16[64,64,32,64]{3,2,1,0:T(8,128)(2,1)} %convert_bitcast_fusion) | data formatting | bytes 33554432 | tf_op jit(solution)/shard_map/convert_element_type | solution.py:164
  (477 shorter events, 1171.6 us)
Async XLA Ops:
  6.5 3.6 copy-start
  6.5 2.3 copy-start.3
  10.8 10.3 copy-start.2
  13.8 55.6 %all-to-all-start = ((bf16[8,8,4,4096]{3,2,1,0:T(4,128)(2,1)}), bf16[8,8,4,4096]{3,2,1,0:T(4,128)(2,1)}, u32[]{:S(2)}, u32[]{:S(2)}) async-start(bf16[8,8,4,4096]{3,2,1,0:T(4,128)(2,1)} %copy.175), calls=%async_computation | async-start | bytes 4194304 | tf_op jit(solution)/shard_map/all_to_all | solution.py:99
  75.2 30.2 %all-to-all-start.1 = ((bf16[4,16,4,4096]{3,1,2,0:T(8,128)(2,1)}), bf16[4,16,4,4096]{3,1,2,0:T(8,128)(2,1)}, u32[]{:S(2)}, u32[]{:S(2)}) async-start(bf16[4,16,4,4096]{3,1,2,0:T(8,128)(2,1)} %convolution_convert_fusion.1), calls=%async_computation.1 | async-start | bytes 4194304 | tf_op jit(solution)/shard_map/all_to_all | solution.py:119
  79.6 265.4 %all-gather.9.cloned.1.call-start = ((), (), s32[]{:S(2)}) async-start(), calls=%async_computation.5 | async-start | bytes 18874368 | tf_op jit(solution)/shard_map/all_gather | solution.py:141
  119.4 283.6 %all-gather.7.cloned.1.call-start = ((), (), s32[]{:S(2)}) async-start(), calls=%async_computation.4 | async-start | bytes 10485760 | tf_op jit(solution)/shard_map/all_gather | solution.py:146
  137.2 7.0 all-to-all-start.3
  140.5 1527.3 %all-gather.11.cloned.1.call-start = ((), (), s32[]{:S(2)}) async-start(), calls=%async_computation.6 | async-start | bytes 10485760 | tf_op jit(solution)/shard_map/all_gather | solution.py:153
  2873.7 46.0 %copy-start.1 = (bf16[8,32,4096]{2,1,0:T(8,128)(2,1)S(1)}, bf16[8,32,4096]{2,1,0:T(8,128)(2,1)}, u32[]{:S(2)}) copy-start(bf16[8,32,4096]{2,1,0:T(8,128)(2,1)} %param.7) | copy-start | bytes 6291460
Sparse Core Ops, SparseCore 0:
  119.5 225.4 all-gather.8
  346.6 56.4 all-gather.6
  1609.5 58.2 all-gather.10
where the time goes:
time: 2960 us; the launch traced here: 2930 us
  local copies, waits for them, and re-layouts  2210 us (75%)
  waiting for transfers between devices  331 us (11%)
  matrix products  268 us (9%)
  other arithmetic  42.8 us (1%)
  blocking collectives  33.6 us (1%)
    broadcast_in_dim x128, local copies, waits for them, and re-layouts, one_group(): jnp.where(hit[:, :, :, :, None], whole_rows[:, :, :, slot][:, :, :, None,...  853 us
    slice x16, local copies, waits for them, and re-layouts, one_group(): whole_rows[:, :, :, slot][:, :, :, None, :]  755 us
    gather x16, local copies, waits for them, and re-layouts, one_group(): whole_rows = far_vals[source]  258 us
    dot_general x16, matrix products, one_group(): jnp.einsum('givab,givubc->iuac', left_factor_blocks, right_factor_blocks,...  238 us
    all_gather x1, waiting for transfers between devices, shards(): lax.all_gather(tile_vals[None], 'col', axis=0, tiled=True)  177 us
    another operation x16, local copies, waits for them, and re-layouts  112 us
    dynamic_slice x16, local copies, waits for them, and re-layouts, filtered_product(): lax.scan(one_group, start, (panel_ids, grouped_vals, grouped_cols))  72.1 us
  transfers between devices with their start and end apart: 6, of which 6 were waited for; matrix products, arithmetic and copies ran while one was open for 2% of the time, Pallas kernels for 0%

commit v1 on v0

--- a/solution.py
+++ b/solution.py
@@ -5,6 +5,18 @@
 from jax.sharding import PartitionSpec as P
 
 BLOCK_EDGE = 64
+
+
+def enter_tokens(panel, mesh_dim):
+    return jnp.concatenate(
+        lax.all_to_all(
+            jnp.stack([panel for _ in range(lax.axis_size(mesh_dim))], axis=0),
+            axis_name=mesh_dim,
+            split_axis=0,
+            concat_axis=0,
+        ),
+        axis=0,
+    )
 
 
 def bucket_slots(x_vals, occupancy, perm, first_row, column_processors, tile_slots):
@@ -138,7 +150,7 @@
     tile_cols = jnp.dot(selector, got_cols + 1) - 1
     cols_wire = tile_cols.astype(jnp.bfloat16)
     row_vals, row_cols = (
-        lax.all_gather(tile_vals[None], "col", axis=0, tiled=True),
+        enter_tokens(tile_vals[None], "col"),
         lax.all_gather(cols_wire[None], "col", axis=0, tiled=True),
     )
     row_cols = row_cols.astype(jnp.int32)

time: 2960 us -> 3070 us (1.037)
  blocking collectives: 33.6 us -> 291 us
  waiting for transfers between devices: 331 us -> 196 us
    all_gather x1, blocking collectives: 17.9 us -> 285 us  [shards(): lax.all_gather(cols_wire[None], 'col', axis=0, tiled=True)]
    all_gather x1 -> x0, waiting for transfers between devices: 177 us -> none  [shards(): lax.all_gather(tile_vals[None], 'col', axis=0, tiled=True)]
    all_to_all x0 -> x2, waiting for transfers between devices: none -> 72.5 us  [the longest x1 71.7 us: enter_tokens(): lax.all_to_all(jnp.stack([panel for _ in range(lax.axis_size(mesh_dim))],...]
    all_gather x1, waiting for transfers between devices: 35.8 us -> 0.02 us  [shards(): lax.all_gather(tile_vals, 'row', axis=0, tiled=True)]
  transfers between devices with their start and end apart: 6 -> 7, of which waited for: 6 -> 5; matrix products, arithmetic and copies ran while one was open for 2% -> 1% of each run, Pallas kernels for 0% -> 0%
where the time goes in v1:
time: 3070 us; the launch traced here: 3040 us
  local copies, waits for them, and re-layouts  2180 us (71%)
  blocking collectives  291 us (9%)
  matrix products  268 us (9%)
  waiting for transfers between devices  196 us (6%)
  other arithmetic  43.7 us (1%)
    broadcast_in_dim x128, local copies, waits for them, and re-layouts, one_group(): jnp.where(hit[:, :, :, :, None], whole_rows[:, :, :, slot][:, :, :, None,...  853 us
    slice x16, local copies, waits for them, and re-layouts, one_group(): whole_rows[:, :, :, slot][:, :, :, None, :]  753 us
    all_gather x1, blocking collectives, shards(): lax.all_gather(cols_wire[None], 'col', axis=0, tiled=True)  285 us
    gather x16, local copies, waits for them, and re-layouts, one_group(): whole_rows = far_vals[source]  258 us
    dot_general x16, matrix products, one_group(): jnp.einsum('givab,givubc->iuac', left_factor_blocks, right_factor_blocks,...  238 us
    another operation x16, local copies, waits for them, and re-layouts  112 us
    all_to_all x1, waiting for transfers between devices, enter_tokens(): lax.all_to_all(jnp.stack([panel for _ in range(lax.axis_size(mesh_dim))],...  71.7 us
    dynamic_slice x16, local copies, waits for them, and re-layouts, filtered_product(): lax.scan(one_group, start, (panel_ids, grouped_vals, grouped_cols))  71.6 us
  transfers between devices with their start and end apart: 7, of which 5 were waited for; matrix products, arithmetic and copies ran while one was open for 1% of the time, Pallas kernels for 0%

profile of v1, /device:TPU:0, one launch (start us, length us, event | category | flops | bytes accessed | tf_op | source)
XLA Modules:
  0.0 3037.8 jit_solution(11395000899656922657)
XLA Ops:
  13.8 7.3 all-to-all-start
  25.2 44.3 %all-to-all-done = bf16[8,8,4,4096]{3,2,1,0:T(4,128)(2,1)} async-done(((bf16[8,8,4,4096]{3,2,1,0:T(4,128)(2,1)}), bf16[8,8,4,4096]{3,2,1,0:T(4,128)(2,1)}, u32[]{:S(2)}, u32[]{:S(2)}) %all-to-all-start) | async-done | bytes 2097184 | tf_op jit(solution)/shard_map/all_to_all | solution.py:111
  85.9 23.9 all-to-all-done.1
  124.4 8.8 stack.3
  140.1 285.5 %all-gather.1 = bf16[8,64,4]{1,2,0:T(4,128)(2,1)S(1)} all-gather(bf16[1,64,4]{1,2,0:T(4,128)(2,1)S(1)} %convert_bitcast_fusion.1), channel_id=2, replica_groups=mesh['row'=4,'col'=8] {'col'}, dimensions={0}, use_global_device_ids=true | all-gather | bytes 4608 | tf_op jit(solution)/shard_map/all_gather | solution.py:154
  431.1 71.7 %all-to-all-done.4 = bf16[8,1,64,4,4096]{4,3,2,1,0:T(4,128)(2,1)} async-done(((bf16[8,1,64,4,4096]{4,3,2,1,0:T(4,128)(2,1)}), bf16[8,1,64,4,4096]{4,3,2,1,0:T(4,128)(2,1)}, u32[]{:S(2)}, u32[]{:S(2)}) %all-to-all-start.4) | async-done | bytes 16777248 | tf_op jit(solution)/shard_map/all_to_all | solution.py:12
  502.8 1186.1 %while.22 = (s32[]{:T(128)}, f32[64,4,64,64]{2,3,1,0:T(8,128)}, s32[8,1,64,4]{3,2,1,0:T(8,128)S(1)}, s32[8,1]{0,1:T(1,128)S(1)}, s32[256,4]{1,0:T(8,128)S(1)}, /...) while((s32[]{:T(128)}, f32[64,4,64,64]{2,3,1,0:T(8,128)}, ...), condition=%wide.region_6.7_spmd.clone, body=%wide.region_5.6_spmd.clone.sunk | while | flops 555760128 | bytes 94430096 | solution.py:90
  521.7 16.1 gather_fusion.1
  537.8 47.0 %slice_reduce_fusion.10 = (bf16[64,4,4096]{2,1,0:T(4,128)(2,1)}, bf16[64,4,4096]{2,1,0:T(4,128)(2,1)}, bf16[64,4,4096]{2,1,0:T(4,128)(2,1)}, bf16[64,4,4096]{2,1,0:T(4,128)(2,1)}) fusion(bf16[1,64,4,4,4096]{4,3,2,1,0:T(4,128)(2,1)} %bitcast.157), kind=kLoop, calls=%fused_computation.23.clone.1 | loop fusion | bytes 16777216 | tf_op jit(solution)/shard_map/while/body/eval_jaxpr/slice | solution.py:70
  649.6 13.5 bitcast_add_fusion.5
  666.6 16.1 gather_fusion.1
  682.7 47.0 %slice_reduce_fusion.10 = (bf16[64,4,4096]{2,1,0:T(4,128)(2,1)}, bf16[64,4,4096]{2,1,0:T(4,128)(2,1)}, bf16[64,4,4096]{2,1,0:T(4,128)(2,1)}, bf16[64,4,4096]{2,1,0:T(4,128)(2,1)}) fusion(bf16[1,64,4,4,4096]{4,3,2,1,0:T(4,128)(2,1)} %bitcast.157), kind=kLoop, calls=%fused_computation.23.clone.1 | loop fusion | bytes 16777216 | tf_op jit(solution)/shard_map/while/body/eval_jaxpr/slice | solution.py:70
  794.5 15.1 bitcast_add_fusion.5
  813.1 16.1 gather_fusion.1
  829.2 47.0 %slice_reduce_fusion.10 = (bf16[64,4,4096]{2,1,0:T(4,128)(2,1)}, bf16[64,4,4096]{2,1,0:T(4,128)(2,1)}, bf16[64,4,4096]{2,1,0:T(4,128)(2,1)}, bf16[64,4,4096]{2,1,0:T(4,128)(2,1)}) fusion(bf16[1,64,4,4,4096]{4,3,2,1,0:T(4,128)(2,1)} %bitcast.157), kind=kLoop, calls=%fused_computation.23.clone.1 | loop fusion | bytes 16777216 | tf_op jit(solution)/shard_map/while/body/eval_jaxpr/slice | solution.py:70
  941.0 15.1 bitcast_add_fusion.5
  959.6 16.1 gather_fusion.1
  975.7 47.0 %slice_reduce_fusion.10 = (bf16[64,4,4096]{2,1,0:T(4,128)(2,1)}, bf16[64,4,4096]{2,1,0:T(4,128)(2,1)}, bf16[64,4,4096]{2,1,0:T(4,128)(2,1)}, bf16[64,4,4096]{2,1,0:T(4,128)(2,1)}) fusion(bf16[1,64,4,4,4096]{4,3,2,1,0:T(4,128)(2,1)} %bitcast.157), kind=kLoop, calls=%fused_computation.23.clone.1 | loop fusion | bytes 16777216 | tf_op jit(solution)/shard_map/while/body/eval_jaxpr/slice | solution.py:70
  1087.5 15.1 bitcast_add_fusion.5
  1106.1 16.1 gather_fusion.1
  1122.2 47.0 %slice_reduce_fusion.10 = (bf16[64,4,4096]{2,1,0:T(4,128)(2,1)}, bf16[64,4,4096]{2,1,0:T(4,128)(2,1)}, bf16[64,4,4096]{2,1,0:T(4,128)(2,1)}, bf16[64,4,4096]{2,1,0:T(4,128)(2,1)}) fusion(bf16[1,64,4,4,4096]{4,3,2,1,0:T(4,128)(2,1)} %bitcast.157), kind=kLoop, calls=%fused_computation.23.clone.1 | loop fusion | bytes 16777216 | tf_op jit(solution)/shard_map/while/body/eval_jaxpr/slice | solution.py:70
  1234.0 15.1 bitcast_add_fusion.5
  1252.5 16.1 gather_fusion.1
  1268.6 47.0 %slice_reduce_fusion.10 = (bf16[64,4,4096]{2,1,0:T(4,128)(2,1)}, bf16[64,4,4096]{2,1,0:T(4,128)(2,1)}, bf16[64,4,4096]{2,1,0:T(4,128)(2,1)}, bf16[64,4,4096]{2,1,0:T(4,128)(2,1)}) fusion(bf16[1,64,4,4,4096]{4,3,2,1,0:T(4,128)(2,1)} %bitcast.157), kind=kLoop, calls=%fused_computation.23.clone.1 | loop fusion | bytes 16777216 | tf_op jit(solution)/shard_map/while/body/eval_jaxpr/slice | solution.py:70
  1380.4 15.1 bitcast_add_fusion.5
  1399.0 16.1 gather_fusion.1
  1415.1 47.0 %slice_reduce_fusion.10 = (bf16[64,4,4096]{2,1,0:T(4,128)(2,1)}, bf16[64,4,4096]{2,1,0:T(4,128)(2,1)}, bf16[64,4,4096]{2,1,0:T(4,128)(2,1)}, bf16[64,4,4096]{2,1,0:T(4,128)(2,1)}) fusion(bf16[1,64,4,4,4096]{4,3,2,1,0:T(4,128)(2,1)} %bitcast.157), kind=kLoop, calls=%fused_computation.23.clone.1 | loop fusion | bytes 16777216 | tf_op jit(solution)/shard_map/while/body/eval_jaxpr/slice | solution.py:70
  1526.9 15.1 bitcast_add_fusion.5
  1545.5 16.1 gather_fusion.1
  1561.6 47.0 %slice_reduce_fusion.10 = (bf16[64,4,4096]{2,1,0:T(4,128)(2,1)}, bf16[64,4,4096]{2,1,0:T(4,128)(2,1)}, bf16[64,4,4096]{2,1,0:T(4,128)(2,1)}, bf16[64,4,4096]{2,1,0:T(4,128)(2,1)}) fusion(bf16[1,64,4,4,4096]{4,3,2,1,0:T(4,128)(2,1)} %bitcast.157), kind=kLoop, calls=%fused_computation.23.clone.1 | loop fusion | bytes 16777216 | tf_op jit(solution)/shard_map/while/body/eval_jaxpr/slice | solution.py:70
  1673.4 15.1 bitcast_add_fusion.5
  1701.7 7.1 convert_element_type.135
  1708.9 7.3 mul.90
  1716.2 9.0 copy.186
  1725.2 55.1 %all-gather.8.cloned.1.call-done = bf16[256,4,4096]{2,1,0:T(4,128)(2,1)} async-done(((bf16[64,4,4096]{2,1,0:T(4,128)(2,1)}), bf16[256,4,4096]{2,1,0:T(4,128)(2,1)}) %all-gather.8.cloned.1.call-update) | async-done | bytes 8388624 | tf_op jit(solution)/shard_map/all_gather | solution.py:165
  1780.3 1170.7 %while.23 = (s32[]{:T(128)}, f32[64,4,64,64]{2,3,1,0:T(8,128)}, s32[8,1,64,4]{3,2,1,0:T(8,128)S(1)}, s32[8,1]{0,1:T(1,128)S(1)}, s32[256,4]{1,0:T(8,128)S(1)}, /...) while((s32[]{:T(128)}, f32[64,4,64,64]{2,3,1,0:T(8,128)}, ...), condition=%wide.region_8.9_spmd.clone, body=%wide.region_7.8_spmd.clone.sunk | while | flops 555760128 | bytes 94430096 | solution.py:90
  1784.0 16.1 gather_fusion.3
  1800.1 47.0 %slice_reduce_fusion.11 = (bf16[64,4,4096]{2,1,0:T(4,128)(2,1)}, bf16[64,4,4096]{2,1,0:T(4,128)(2,1)}, bf16[64,4,4096]{2,1,0:T(4,128)(2,1)}, bf16[64,4,4096]{2,1,0:T(4,128)(2,1)}) fusion(bf16[1,64,4,4,4096]{4,3,2,1,0:T(4,128)(2,1)} %bitcast.158), kind=kLoop, calls=%fused_computation.53.clone.1 | loop fusion | bytes 16777216 | tf_op jit(solution)/shard_map/while/body/eval_jaxpr/slice | solution.py:70
  1911.9 13.5 bitcast_add_fusion.6
  1928.9 16.1 gather_fusion.3
  1945.0 47.0 %slice_reduce_fusion.11 = (bf16[64,4,4096]{2,1,0:T(4,128)(2,1)}, bf16[64,4,4096]{2,1,0:T(4,128)(2,1)}, bf16[64,4,4096]{2,1,0:T(4,128)(2,1)}, bf16[64,4,4096]{2,1,0:T(4,128)(2,1)}) fusion(bf16[1,64,4,4,4096]{4,3,2,1,0:T(4,128)(2,1)} %bitcast.158), kind=kLoop, calls=%fused_computation.53.clone.1 | loop fusion | bytes 16777216 | tf_op jit(solution)/shard_map/while/body/eval_jaxpr/slice | solution.py:70
  2056.8 15.1 bitcast_add_fusion.6
  2075.4 16.1 gather_fusion.3
  2091.5 47.0 %slice_reduce_fusion.11 = (bf16[64,4,4096]{2,1,0:T(4,128)(2,1)}, bf16[64,4,4096]{2,1,0:T(4,128)(2,1)}, bf16[64,4,4096]{2,1,0:T(4,128)(2,1)}, bf16[64,4,4096]{2,1,0:T(4,128)(2,1)}) fusion(bf16[1,64,4,4,4096]{4,3,2,1,0:T(4,128)(2,1)} %bitcast.158), kind=kLoop, calls=%fused_computation.53.clone.1 | loop fusion | bytes 16777216 | tf_op jit(solution)/shard_map/while/body/eval_jaxpr/slice | solution.py:70
  2203.3 15.1 bitcast_add_fusion.6
  2221.9 16.1 gather_fusion.3
  2238.1 47.0 %slice_reduce_fusion.11 = (bf16[64,4,4096]{2,1,0:T(4,128)(2,1)}, bf16[64,4,4096]{2,1,0:T(4,128)(2,1)}, bf16[64,4,4096]{2,1,0:T(4,128)(2,1)}, bf16[64,4,4096]{2,1,0:T(4,128)(2,1)}) fusion(bf16[1,64,4,4,4096]{4,3,2,1,0:T(4,128)(2,1)} %bitcast.158), kind=kLoop, calls=%fused_computation.53.clone.1 | loop fusion | bytes 16777216 | tf_op jit(solution)/shard_map/while/body/eval_jaxpr/slice | solution.py:70
  2349.9 15.1 bitcast_add_fusion.6
  2368.4 16.1 gather_fusion.3
  2384.5 47.0 %slice_reduce_fusion.11 = (bf16[64,4,4096]{2,1,0:T(4,128)(2,1)}, bf16[64,4,4096]{2,1,0:T(4,128)(2,1)}, bf16[64,4,4096]{2,1,0:T(4,128)(2,1)}, bf16[64,4,4096]{2,1,0:T(4,128)(2,1)}) fusion(bf16[1,64,4,4,4096]{4,3,2,1,0:T(4,128)(2,1)} %bitcast.158), kind=kLoop, calls=%fused_computation.53.clone.1 | loop fusion | bytes 16777216 | tf_op jit(solution)/shard_map/while/body/eval_jaxpr/slice | solution.py:70
  2496.3 15.1 bitcast_add_fusion.6
  2514.9 16.1 gather_fusion.3
  2531.0 47.0 %slice_reduce_fusion.11 = (bf16[64,4,4096]{2,1,0:T(4,128)(2,1)}, bf16[64,4,4096]{2,1,0:T(4,128)(2,1)}, bf16[64,4,4096]{2,1,0:T(4,128)(2,1)}, bf16[64,4,4096]{2,1,0:T(4,128)(2,1)}) fusion(bf16[1,64,4,4,4096]{4,3,2,1,0:T(4,128)(2,1)} %bitcast.158), kind=kLoop, calls=%fused_computation.53.clone.1 | loop fusion | bytes 16777216 | tf_op jit(solution)/shard_map/while/body/eval_jaxpr/slice | solution.py:70
  2642.8 15.1 bitcast_add_fusion.6
  2661.4 16.1 gather_fusion.3
  2677.5 47.0 %slice_reduce_fusion.11 = (bf16[64,4,4096]{2,1,0:T(4,128)(2,1)}, bf16[64,4,4096]{2,1,0:T(4,128)(2,1)}, bf16[64,4,4096]{2,1,0:T(4,128)(2,1)}, bf16[64,4,4096]{2,1,0:T(4,128)(2,1)}) fusion(bf16[1,64,4,4,4096]{4,3,2,1,0:T(4,128)(2,1)} %bitcast.158), kind=kLoop, calls=%fused_computation.53.clone.1 | loop fusion | bytes 16777216 | tf_op jit(solution)/shard_map/while/body/eval_jaxpr/slice | solution.py:70
  2789.3 15.1 bitcast_add_fusion.6
  2807.9 16.1 gather_fusion.3
  2824.0 47.0 %slice_reduce_fusion.11 = (bf16[64,4,4096]{2,1,0:T(4,128)(2,1)}, bf16[64,4,4096]{2,1,0:T(4,128)(2,1)}, bf16[64,4,4096]{2,1,0:T(4,128)(2,1)}, bf16[64,4,4096]{2,1,0:T(4,128)(2,1)}) fusion(bf16[1,64,4,4,4096]{4,3,2,1,0:T(4,128)(2,1)} %bitcast.158), kind=kLoop, calls=%fused_computation.53.clone.1 | loop fusion | bytes 16777216 | tf_op jit(solution)/shard_map/while/body/eval_jaxpr/slice | solution.py:70
  2935.8 15.1 bitcast_add_fusion.6
  2951.0 10.0 multiply_subtract_fusion
  2961.0 7.5 copy.188
  2968.5 16.1 convert_bitcast_fusion
  2984.5 46.0 %convert_element_type.138 = bf16[4096,2048]{1,0:T(8,128)(2,1)} reshape(bf16[64,64,32,64]{3,2,1,0:T(8,128)(2,1)} %convert_bitcast_fusion) | data formatting | bytes 33554432 | tf_op jit(solution)/shard_map/convert_element_type | solution.py:176
  (477 shorter events, 1159.3 us)
Async XLA Ops:
  6.5 3.6 copy-start
  6.5 2.3 copy-start.4
  10.8 10.3 copy-start.2
  13.8 55.7 %all-to-all-start = ((bf16[8,8,4,4096]{3,2,1,0:T(4,128)(2,1)}), bf16[8,8,4,4096]{3,2,1,0:T(4,128)(2,1)}, u32[]{:S(2)}, u32[]{:S(2)}) async-start(bf16[8,8,4,4096]{3,2,1,0:T(4,128)(2,1)} %copy.172), calls=%async_computation | async-start | bytes 4194304 | tf_op jit(solution)/shard_map/all_to_all | solution.py:111
  69.4 10.2 all-to-all-start.2
  79.6 30.2 all-to-all-start.1
  109.8 14.6 all-to-all-start.3
  124.4 8.8 copy-start.3
  133.2 369.5 %all-to-all-start.4 = ((bf16[8,1,64,4,4096]{4,3,2,1,0:T(4,128)(2,1)}), bf16[8,1,64,4,4096]{4,3,2,1,0:T(4,128)(2,1)}, u32[]{:S(2)}, u32[]{:S(2)}) async-start(bf16[8,1,64,4,4096]{4,3,2,1,0:T(4,128)(2,1)} %stack.3), calls=%async_computation.4 | async-start | bytes 33554432 | tf_op jit(solution)/shard_map/all_to_all | solution.py:12
  139.0 292.1 %all-gather.6.cloned.1.call-start = ((), (), s32[]{:S(2)}) async-start(), calls=%async_computation.5 | async-start | bytes 10485760 | tf_op jit(solution)/shard_map/all_gather | solution.py:158
  139.7 1640.6 %all-gather.8.cloned.1.call-start = ((), (), s32[]{:S(2)}) async-start(), calls=%async_computation.6 | async-start | bytes 10485760 | tf_op jit(solution)/shard_map/all_gather | solution.py:165
  2984.5 46.0 %copy-start.1 = (bf16[8,32,4096]{2,1,0:T(8,128)(2,1)S(1)}, bf16[8,32,4096]{2,1,0:T(8,128)(2,1)}, u32[]{:S(2)}) copy-start(bf16[8,32,4096]{2,1,0:T(8,128)(2,1)} %param.7) | copy-start | bytes 6291460
Sparse Core Ops, SparseCore 0:
  141.3 60.0 all-gather.5
  1709.0 71.2 all-gather.7
